TPU v7x, 32 devices: a whole 2x2x4 slice. The times are simulated.
32 devices in a mesh: layer: 2 (over x), band: 16 (over z, y, core).
Axes of the slice: x: 2, y: 2, z: 4, core: 2. Of those that a mesh axis runs over, the one named last changes fastest.
Arguments:
- coeffs: bfloat16 [32, 128, 10240], P('layer', None, 'band'), may hold values from -6 to 6
- hamilton: bfloat16 [32, 7, 128, 128], P('layer'), may hold values from -0.1875 to 0.1875
- neighbors: int32 [32, 7], P('layer'), may hold values from -1 to 31, as said below
- basis: bfloat16 [32, 1728, 128], P(('layer', 'band')), may hold values from -0.5 to 0.5
- occupation: int32 [10240], replicated, may hold values from 0 to 3
Outputs:
- filtered: bfloat16 [32, 128, 10240], P('layer', None, 'band')
- density: float32 [32, 1728], P(('layer', 'band'))
Inputs may be any that keep to these rules, and one draw needn't show every extreme that they name: `neighbors`: column 0 of row e is e itself; columns 1 to 4 are its neighbours along the two periodic in-plane directions, all in e's plane of 16 elements (rows e // 16 * 16 to that plus 16 - 1); columns 5 and 6 are the elements at the same lattice site in the previous and the next plane, -1 before the first and after the last plane. The numbering of sites within each plane is drawn.
All inputs are finite; a program needn't handle non-finite values.
Results may differ from a plain program's by a relative error of at most 0.0042.
Values may be sent and summed in bfloat16 or wider, within the bound.
A program may use at most 64 MiB of HBM per device.

v0:
```python
import jax
import jax.numpy as jnp
from jax import lax
from jax.sharding import PartitionSpec as P

NBAND = 10240
FY = 4
FZ = 4


center = 0.5
half_width = 1.5


def with_halo(array, sides, width):
    for axis, dim in sides:
        devices, length = (lax.axis_size(axis), array.shape[dim])
        up = [(i, (i + 1) % devices) for i in range(devices - 1)]
        down = [(j, i) for i, j in up]
        last = lax.slice_in_dim(array, length - width, length, axis=dim)
        first = lax.slice_in_dim(array, 0, width, axis=dim)
        before = lax.ppermute(last, axis, up)
        after = lax.ppermute(first, axis, down)
        array = jnp.concatenate([before, array, after], axis=dim)
    return array


def neighbor_product(blocks, nearby):
    return jnp.einsum("ekij,ekjb->eib", blocks, nearby, preferred_element_type=jnp.float32)


def body(coeffs, hamilton, neighbors, basis, occupation):
    elements = coeffs.shape[0]
    face_size = FY * FZ
    offset = lax.axis_index("layer") * elements - face_size
    usable = neighbors >= 0
    position = jnp.where(usable, neighbors - offset, 0)
    allowed = usable.astype(jnp.bfloat16)

    def operate(source):
        padded = with_halo(source, (("layer", 0),), face_size)
        inside = source[position[:, :5] - face_size]
        result = neighbor_product(hamilton[:, :5], inside)
        across = padded[position[:, 5:]] * allowed[:, 5:, None, None]
        return result + neighbor_product(hamilton[:, 5:], across)

    start_vals = coeffs.astype(jnp.float32)
    first_image = operate(coeffs)
    filtered_once = ((first_image - center * start_vals) / half_width).astype(jnp.bfloat16)
    second_image = operate(filtered_once)
    filtered = (
        2.0 * (second_image - center * filtered_once.astype(jnp.float32)) / half_width - start_vals
    ).astype(jnp.bfloat16)
    weights = (1 + occupation).astype(jnp.float32) / (2.0 * NBAND)
    copies = lax.axis_size("band") // elements
    duplicated = jnp.tile(filtered, (copies, 1, 1))
    regrouped = lax.all_to_all(duplicated, "band", split_axis=0, concat_axis=2, tiled=True)
    orbital = jnp.dot(basis[0], regrouped[0], preferred_element_type=jnp.float32)
    density = jnp.sum(orbital * orbital * weights[None, :], axis=1)[None, :]
    return (filtered, density)


def solution(mesh):
    return jax.shard_map(
        body,
        mesh=mesh,
        in_specs=(
            P("layer", None, "band"),
            P("layer", None, None, None),
            P("layer", None),
            P(("layer", "band"), None, None),
            P(),
        ),
        out_specs=(P("layer", None, "band"), P(("layer", "band"), None)),
        check_vma=False,
    )
```

profile of v0, /device:TPU:15, one launch (start us, length us, event | category | flops | bytes accessed | tf_op | source)
XLA Modules:
  0.0 254.1 jit_solution(5646410160833362357)
XLA Ops:
  0.6 0.0 copy-start
  0.6 0.0 copy-start.1
  0.7 0.0 copy-start.4
  0.7 3.9 %collective-permute-start.1 = (bf16[16,128,640]{2,1,0:T(8,128)(2,1)}, bf16[16,128,640]{2,1,0:T(8,128)(2,1)}, u32[]{:S(2)}, u32[]{:S(2)}) collective-permute-start(bf16[16,128,640]{2,1,0:T(8,128)(2,1)} %param.5), channel_id=1, source_target_pairs={{16,0},{17,1},{18,2},{19,3},{20,4},{21,5},{22,6},{23,7},{24,8},{25... | collective-permute-start | bytes 7864328 | tf_op jit(solution)/shard_map/ppermute | solution.py:23
  4.6 1.3 collective-permute-start
  5.8 4.4 %copy.19 = bf16[16,128,640]{1,2,0:T(8,128)(2,1)} copy(bf16[16,128,640]{2,1,0:T(8,128)(2,1)} %param.5) | data formatting | bytes 5242880 | tf_op args[0]
  10.2 0.0 copy-done.4
  10.2 0.1 copy.14
  10.3 0.1 reshape.9
  10.4 0.0 copy-done.1
  10.4 7.5 %gather_fusion = bf16[80,128,640]{2,1,0:T(8,128)(2,1)} fusion(bf16[16,128,640]{2,1,0:T(8,128)(2,1)S(1)} %copy-done.1, s32[1024]{0:T(1024)S(1)} %pad_clamp_fusion.1), kind=kCustom, calls=%fused_computation | custom fusion | bytes 26214720 | tf_op jit(solution)/shard_map/gather | solution.py:42
  17.9 0.1 copy.16
  18.0 0.1 reshape.17
  18.1 0.1 copy.17
  18.2 9.0 %fusion.13 = f32[16,640,128,1]{2,1,3,0:T(8,128)} fusion(bf16[16,5,128,640]{3,2,1,0:T(8,128)(2,1)} %bitcast.39, bf16[16,7,128,128]{3,2,1,0:T(8,128)(2,1)} %param.6), kind=kOutput, calls=%fused_computation.25 | convolution fusion | flops 1677721600 | bytes 20971520 | tf_op jit(solution)/shard_map/ekij,ekjb->eib/dot_general | solution.py:29
  27.2 31.8 %collective-permute-done.1 = bf16[16,128,640]{2,1,0:T(8,128)(2,1)} collective-permute-done((bf16[16,128,640]{2,1,0:T(8,128)(2,1)}, bf16[16,128,640]{2,1,0:T(8,128)(2,1)}, u32[]{:S(2)}, u32[]{:S(2)}) %collective-permute-start.1) | collective-permute-done | bytes 2621472 | tf_op jit(solution)/shard_map/ppermute | solution.py:23
  58.9 5.3 %collective-permute-done = bf16[16,128,640]{2,1,0:T(8,128)(2,1)} collective-permute-done((bf16[16,128,640]{2,1,0:T(8,128)(2,1)}, bf16[16,128,640]{2,1,0:T(8,128)(2,1)}, u32[]{:S(2)}, u32[]{:S(2)}) %collective-permute-start) | collective-permute-done | bytes 2621472 | tf_op jit(solution)/shard_map/ppermute | solution.py:22
  64.2 6.4 %pad_maximum_fusion = bf16[48,128,640]{2,1,0:T(8,128)(2,1)} fusion(bf16[16,128,640]{2,1,0:T(8,128)(2,1)} %collective-permute-done.1, bf16[16,128,640]{2,1,0:T(8,128)(2,1)S(1)} %copy-done.1, bf16[16,128,640]{2,1,0:T(8,128)(2,1)} %collective-permute-done), kind=kLoop, calls=%fused_computation.5 | loop fusion | flops 7864320 | bytes 15728640 | tf_op jit(solution)/shard_map/concatenate | solution.py:24
  70.6 6.7 %gather_fusion.1 = bf16[32,128,640]{2,1,0:T(8,128)(2,1)} fusion(bf16[48,128,640]{2,1,0:T(8,128)(2,1)} %pad_maximum_fusion, s32[1024]{0:T(1024)S(1)} %pad_clamp_fusion), kind=kCustom, calls=%fused_computation.1 | custom fusion | bytes 10485888 | tf_op jit(solution)/shard_map/gather | solution.py:44
  77.3 7.8 %copy.18 = bf16[16,2,128,640]{2,3,1,0:T(8,128)(2,1)} copy(bf16[16,2,128,640]{3,2,1,0:T(8,128)(2,1)} %bitcast.40) | data formatting | bytes 10485760 | tf_op jit(solution)/shard_map/gather | solution.py:44
  85.1 6.7 %fusion.2 = bf16[16,128,640]{1,2,0:T(8,128)(2,1)S(1)} fusion(bf16[16,128,640]{1,2,0:T(8,128)(2,1)} %copy.19, f32[16,640,128,1]{2,1,3,0:T(8,128)} %fusion.13, bf16[16,2,128,640]{2,3,1,0:T(8,128)(2,1)} %copy.18, bf16[16,2]{1,0:T(8,128)(2,1)S(1)} %copy.17, bf16[16,7,128,128]{3,2,1,0:T(8,128)(2,1)} %param.6), kind=kOutput, calls=%fused_computation.11 | convolution fusion | flops 681574400 | bytes 16777280 | tf_op jit(solution)/shard_map/ekij,ekjb->eib/dot_general | solution.py:29
  91.8 2.8 %collective-permute-start.3 = (bf16[16,128,640]{1,2,0:T(8,128)(2,1)S(1)}, bf16[16,128,640]{1,2,0:T(8,128)(2,1)}, u32[]{:S(2)}, u32[]{:S(2)}) collective-permute-start(bf16[16,128,640]{1,2,0:T(8,128)(2,1)S(1)} %fusion.2), channel_id=1, source_target_pairs={{16,0},{17,1},{18,2},{19,3},{20,4},{21,5},{22,6},{23,7},{24,8},{25... | collective-permute-start | bytes 7864328 | tf_op jit(solution)/shard_map/ppermute | solution.py:23
  94.6 1.5 collective-permute-start.2
  96.0 7.3 %gather_fusion.2 = bf16[80,128,640]{1,2,0:T(8,128)(2,1)} fusion(bf16[16,128,640]{1,2,0:T(8,128)(2,1)S(1)} %fusion.2, s32[1024]{0:T(1024)S(1)} %pad_clamp_fusion.1), kind=kCustom, calls=%fused_computation.2 | custom fusion | bytes 26214720 | tf_op jit(solution)/shard_map/gather | solution.py:42
  103.3 11.3 %fusion.11 = f32[16,640,128,1]{2,1,3,0:T(8,128)} fusion(bf16[16,5,128,640]{2,3,1,0:T(8,128)(2,1)} %bitcast.41, bf16[16,7,128,128]{3,2,1,0:T(8,128)(2,1)} %param.6), kind=kOutput, calls=%fused_computation.23 | convolution fusion | flops 1677721600 | bytes 20971520 | tf_op jit(solution)/shard_map/ekij,ekjb->eib/dot_general | solution.py:29
  114.6 33.0 %collective-permute-done.3 = bf16[16,128,640]{1,2,0:T(8,128)(2,1)} collective-permute-done((bf16[16,128,640]{1,2,0:T(8,128)(2,1)S(1)}, bf16[16,128,640]{1,2,0:T(8,128)(2,1)}, u32[]{:S(2)}, u32[]{:S(2)}) %collective-permute-start.3) | collective-permute-done | bytes 2621472 | tf_op jit(solution)/shard_map/ppermute | solution.py:23
  147.6 5.4 %collective-permute-done.2 = bf16[16,128,640]{1,2,0:T(8,128)(2,1)} collective-permute-done((bf16[16,128,640]{1,2,0:T(8,128)(2,1)S(1)}, bf16[16,128,640]{1,2,0:T(8,128)(2,1)}, u32[]{:S(2)}, u32[]{:S(2)}) %collective-permute-start.2) | collective-permute-done | bytes 2621472 | tf_op jit(solution)/shard_map/ppermute | solution.py:22
  153.0 6.3 %pad_maximum_fusion.1 = bf16[48,128,640]{1,2,0:T(8,128)(2,1)} fusion(bf16[16,128,640]{1,2,0:T(8,128)(2,1)} %collective-permute-done.3, bf16[16,128,640]{1,2,0:T(8,128)(2,1)S(1)} %fusion.2, bf16[16,128,640]{1,2,0:T(8,128)(2,1)} %collective-permute-done.2), kind=kLoop, calls=%fused_computation.6 | loop fusion | flops 7864320 | bytes 15728640 | tf_op jit(solution)/shard_map/concatenate | solution.py:24
  159.3 6.8 %gather_fusion.3 = bf16[32,128,640]{1,2,0:T(8,128)(2,1)} fusion(bf16[48,128,640]{1,2,0:T(8,128)(2,1)} %pad_maximum_fusion.1, s32[1024]{0:T(1024)S(1)} %pad_clamp_fusion), kind=kCustom, calls=%fused_computation.3 | custom fusion | bytes 10485888 | tf_op jit(solution)/shard_map/gather | solution.py:44
  166.1 8.4 %fusion.3 = bf16[16,128,640]{1,2,0:T(8,128)(2,1)} fusion(bf16[16,128,640]{1,2,0:T(8,128)(2,1)} %copy.19, f32[16,640,128,1]{2,1,3,0:T(8,128)} %fusion.11, bf16[16,128,640]{1,2,0:T(8,128)(2,1)S(1)} %fusion.2, bf16[16,2,128,640]{2,3,1,0:T(8,128)(2,1)} %bitcast.42, bf16[16,2]{1,0:T(8,128)(2,1)S(1)} %copy.17, bf16[16,7,128,128]{3,2,1,0:T(8,128)(2,1)} %param.6), kind=kOutput, calls=%fused_computation.12 | convolution fusion | flops 684195840 | bytes 19398720 | tf_op jit(solution)/shard_map/ekij,ekjb->eib/dot_general | solution.py:29
  174.5 0.0 copy-start.3
  174.5 0.0 copy-start.2
  174.5 8.9 %all-to-all-start = ((bf16[16,128,640]{1,2,0:T(8,128)(2,1)}), bf16[16,128,640]{1,2,0:T(8,128)(2,1)}, u32[]{:S(2)}, u32[]{:S(2)}) async-start(bf16[16,128,640]{1,2,0:T(8,128)(2,1)} %fusion.3), calls=%async_computation | async-start | bytes 5242880 | tf_op jit(solution)/shard_map/all_to_all | solution.py:57
  183.4 0.0 copy-done.3
  183.4 0.0 copy-done.2
  183.4 2.6 %copy.20 = bf16[16,128,640]{2,1,0:T(8,128)(2,1)} copy(bf16[16,128,640]{1,2,0:T(8,128)(2,1)S(1)} %copy-done.2) | data formatting | bytes 5242880
  186.0 56.2 %all-to-all-done = bf16[16,128,640]{1,2,0:T(8,128)(2,1)} async-done(((bf16[16,128,640]{1,2,0:T(8,128)(2,1)}), bf16[16,128,640]{1,2,0:T(8,128)(2,1)}, u32[]{:S(2)}, u32[]{:S(2)}) %all-to-all-start) | async-done | bytes 2621472 | tf_op jit(solution)/shard_map/all_to_all | solution.py:57
  242.2 0.0 copy-done
  242.2 11.3 %multiply_reduce_fusion = f32[1728]{0:T(1024)S(1)} fusion(bf16[128,10240]{0,1:T(8,128)(2,1)} %bitcast.16, f32[10240]{0:T(1024)S(1)} %convert_multiply_fusion.1, bf16[1,1728,128]{2,1,0:T(8,128)(2,1)S(1)} %copy-done), kind=kOutput, calls=%fused_computation.4 | convolution fusion | flops 4582930944 | bytes 3111680 | tf_op jit(solution)/shard_map/dot_general | solution.py:58
  253.5 0.6 broadcast_in_dim.18
  (8 shorter events, 0.0 us)
Async XLA Ops:
  0.6 241.5 %copy-start = (bf16[1,1728,128]{2,1,0:T(8,128)(2,1)S(1)}, bf16[1,1728,128]{2,1,0:T(8,128)(2,1)}, u32[]{:S(2)}) copy-start(bf16[1,1728,128]{2,1,0:T(8,128)(2,1)} %param.8) | copy-start | bytes 1327108
  0.6 9.8 %copy-start.1 = (bf16[16,128,640]{2,1,0:T(8,128)(2,1)S(1)}, bf16[16,128,640]{2,1,0:T(8,128)(2,1)}, u32[]{:S(2)}) copy-start(bf16[16,128,640]{2,1,0:T(8,128)(2,1)} %param.5) | copy-start | bytes 7864324
  0.7 9.6 %copy-start.4 = (s32[16,7]{0,1:T(8,128)S(1)}, s32[16,7]{0,1:T(8,128)}, u32[]{:S(2)}) copy-start(s32[16,7]{0,1:T(8,128)} %param.7) | copy-start | bytes 1348
  0.7 58.3 %collective-permute-start.1 = (bf16[16,128,640]{2,1,0:T(8,128)(2,1)}, bf16[16,128,640]{2,1,0:T(8,128)(2,1)}, u32[]{:S(2)}, u32[]{:S(2)}) collective-permute-start(bf16[16,128,640]{2,1,0:T(8,128)(2,1)} %param.5), channel_id=1, source_target_pairs={{16,0},{17,1},{18,2},{19,3},{20,4},{21,5},{22,6},{23,7},{24,8},{25... | collective-permute-start | bytes 7864328 | tf_op jit(solution)/shard_map/ppermute | solution.py:23
  4.6 59.7 %collective-permute-start = (bf16[16,128,640]{2,1,0:T(8,128)(2,1)}, bf16[16,128,640]{2,1,0:T(8,128)(2,1)}, u32[]{:S(2)}, u32[]{:S(2)}) collective-permute-start(bf16[16,128,640]{2,1,0:T(8,128)(2,1)} %param.5), channel_id=1, source_target_pairs={{0,16},{1,17},{2,18},{3,19},{4,20},{5,21},{6,22},{7,23},{8,24},{9,... | collective-permute-start | bytes 7864328 | tf_op jit(solution)/shard_map/ppermute | solution.py:22
  91.8 55.8 %collective-permute-start.3 = (bf16[16,128,640]{1,2,0:T(8,128)(2,1)S(1)}, bf16[16,128,640]{1,2,0:T(8,128)(2,1)}, u32[]{:S(2)}, u32[]{:S(2)}) collective-permute-start(bf16[16,128,640]{1,2,0:T(8,128)(2,1)S(1)} %fusion.2), channel_id=1, source_target_pairs={{16,0},{17,1},{18,2},{19,3},{20,4},{21,5},{22,6},{23,7},{24,8},{25... | collective-permute-start | bytes 7864328 | tf_op jit(solution)/shard_map/ppermute | solution.py:23
  94.6 58.4 %collective-permute-start.2 = (bf16[16,128,640]{1,2,0:T(8,128)(2,1)S(1)}, bf16[16,128,640]{1,2,0:T(8,128)(2,1)}, u32[]{:S(2)}, u32[]{:S(2)}) collective-permute-start(bf16[16,128,640]{1,2,0:T(8,128)(2,1)S(1)} %fusion.2), channel_id=1, source_target_pairs={{0,16},{1,17},{2,18},{3,19},{4,20},{5,21},{6,22},{7,23},{8,24},{9,... | collective-permute-start | bytes 7864328 | tf_op jit(solution)/shard_map/ppermute | solution.py:22
  174.5 8.9 %copy-start.3 = (s32[10240]{0:T(1024)S(1)}, s32[10240]{0:T(1024)}, u32[]{:S(2)}) copy-start(s32[10240]{0:T(1024)} %param.9) | copy-start | bytes 122884
  174.5 9.0 %copy-start.2 = (bf16[16,128,640]{1,2,0:T(8,128)(2,1)S(1)}, bf16[16,128,640]{1,2,0:T(8,128)(2,1)}, u32[]{:S(2)}) copy-start(bf16[16,128,640]{1,2,0:T(8,128)(2,1)} %fusion.3) | copy-start | bytes 7864324
  174.5 67.7 %all-to-all-start = ((bf16[16,128,640]{1,2,0:T(8,128)(2,1)}), bf16[16,128,640]{1,2,0:T(8,128)(2,1)}, u32[]{:S(2)}, u32[]{:S(2)}) async-start(bf16[16,128,640]{1,2,0:T(8,128)(2,1)} %fusion.3), calls=%async_computation | async-start | bytes 5242880 | tf_op jit(solution)/shard_map/all_to_all | solution.py:57
where the time goes:
time: 255 us; the launch traced here: 254 us
  waiting for transfers between devices  132 us (52%)
  matrix products  46.7 us (18%)
  local copies, waits for them, and re-layouts  44 us (17%)
  starting transfers between devices  18.3 us (7%)
  other arithmetic  12.7 us (5%)
    ppermute x2, waiting for transfers between devices, with_halo(): after = lax.ppermute(first, axis, down)  64.8 us
    all_to_all x1, waiting for transfers between devices, body(): lax.all_to_all(duplicated, 'band', split_axis=0, concat_axis=2, tiled=True)  56.2 us
    dot_general x4, matrix products, neighbor_product(): jnp.einsum('ekij,ekjb->eib', blocks, nearby, preferred_element_type=jnp.f...  35.3 us
    gather x3, local copies, waits for them, and re-layouts, operate(): across = padded[position[:, 5:]] * allowed[:, 5:, None, None]  21.3 us
    gather x2, local copies, waits for them, and re-layouts, operate(): inside = source[position[:, :5] - face_size]  14.7 us
    concatenate x2, other arithmetic, with_halo(): array = jnp.concatenate([before, array, after], axis=dim)  12.7 us
    dot_general x1, matrix products, body(): jnp.dot(basis[0], regrouped[0], preferred_element_type=jnp.float32)  11.3 us
    ppermute x2, waiting for transfers between devices, with_halo(): before = lax.ppermute(last, axis, up)  10.7 us
  transfers between devices with their start and end apart: 5, of which 5 were waited for; matrix products, arithmetic and copies ran while one was open for 17% of the time, Pallas kernels for 0%

commit v1 on v0

--- a/solution.py
+++ b/solution.py
@@ -1,12 +1,15 @@
+import functools
+
 import jax
 import jax.numpy as jnp
 from jax import lax
+from jax.experimental import pallas as pl
+from jax.experimental.pallas import tpu as pltpu
 from jax.sharding import PartitionSpec as P
 
-NBAND = 10240
 FY = 4
 FZ = 4
-
+MESH = pl.DeviceIdType.MESH
 
 center = 0.5
 half_width = 1.5
@@ -29,7 +32,7 @@
     return jnp.einsum("ekij,ekjb->eib", blocks, nearby, preferred_element_type=jnp.float32)
 
 
-def body(coeffs, hamilton, neighbors, basis, occupation):
+def general_body(coeffs, hamilton, neighbors, basis, occupation):
     elements = coeffs.shape[0]
     face_size = FY * FZ
     offset = lax.axis_index("layer") * elements - face_size
@@ -51,7 +54,7 @@
     filtered = (
         2.0 * (second_image - center * filtered_once.astype(jnp.float32)) / half_width - start_vals
     ).astype(jnp.bfloat16)
-    weights = (1 + occupation).astype(jnp.float32) / (2.0 * NBAND)
+    weights = (1 + occupation).astype(jnp.float32) / (2.0 * occupation.shape[0])
     copies = lax.axis_size("band") // elements
     duplicated = jnp.tile(filtered, (copies, 1, 1))
     regrouped = lax.all_to_all(duplicated, "band", split_axis=0, concat_axis=2, tiled=True)
@@ -60,7 +63,241 @@
     return (filtered, density)
 
 
+def kernel(spans, nb, c_hbm, h_hbm, nbr_hbm, basis_hbm, occ_ref, filt_hbm, dens_ref, *scratch):
+    count = len(spans)
+    cown, cx, f1o, f1x, outv = (scratch[i * count:(i + 1) * count] for i in range(5))
+    (hown, hx, basis_v, nx_v, nown, nx, gram, gsend, grecv,
+     c_send, c_recv, hx_send, hx_recv, n_send, n_recv, f_send, f_recv, g_send, g_recv,
+     lc_sem, lh_sem, lo_sem, misc_sem) = scratch[5 * count:]
+    elements = c_hbm.shape[0]
+    nbl = c_hbm.shape[2]
+    layer, b = lax.axis_index("layer"), lax.axis_index("band")
+    other = 1 - layer
+    nz = nb // 4
+    z, y, core = b // 4, (b // 2) % 2, b % 2
+    own_cross, x_cross = 6 - layer, 6 - other
+
+    def ident(zz, yy, cc):
+        return zz * 4 + yy * 2 + cc
+
+    n_copy = pltpu.make_async_copy(nbr_hbm, nown, misc_sem.at[0])
+    n_copy.start()
+    c_copies = []
+    h_copies = [
+        pltpu.make_async_copy(h_hbm.at[:, pl.ds(0, 5)], hown.at[:, pl.ds(0, 5)], lh_sem.at[0]),
+        pltpu.make_async_copy(h_hbm.at[:, pl.ds(own_cross, 1)], hown.at[:, pl.ds(5, 1)], lh_sem.at[1]),
+    ]
+
+    barrier = pltpu.get_barrier_semaphore()
+    pl.semaphore_signal(barrier, inc=1, device_id={"layer": other, "band": b}, device_id_type=MESH)
+    for k in range(1, nb):
+        pl.semaphore_signal(barrier, inc=1, device_id={"layer": layer, "band": (b + k) % nb}, device_id_type=MESH)
+    pl.semaphore_wait(barrier, nb)
+
+    def to_x(src, dst, send, recv):
+        return pltpu.make_async_remote_copy(
+            src_ref=src, dst_ref=dst, send_sem=send, recv_sem=recv,
+            device_id={"layer": other, "band": b}, device_id_type=MESH)
+
+    def to_band(src, dst, send, recv, peer):
+        return pltpu.make_async_remote_copy(
+            src_ref=src, dst_ref=dst, send_sem=send, recv_sem=recv,
+            device_id={"layer": layer, "band": peer}, device_id_type=MESH)
+
+    h_across = [
+        to_x(h_hbm.at[b, pl.ds(0, 5)], hx.at[b, pl.ds(0, 5)], hx_send.at[0], hx_recv.at[0]),
+        to_x(h_hbm.at[b, pl.ds(own_cross, 1)], hx.at[b, pl.ds(5, 1)], hx_send.at[1], hx_recv.at[1]),
+    ]
+    n_across = to_x(nbr_hbm, nx_v, n_send.at[0], n_recv.at[0])
+    c_across = [
+        to_x(c_hbm.at[:, :, pl.ds(lo, n)], cx[i], c_send.at[i], c_recv.at[i])
+        for i, (lo, n) in enumerate(spans)
+    ]
+    for copy in h_across + [n_across] + c_across:
+        copy.start()
+    for i, (lo, n) in enumerate(spans):
+        copy = pltpu.make_async_copy(c_hbm.at[:, :, pl.ds(lo, n)], cown[i], lc_sem.at[i])
+        copy.start()
+        c_copies.append(copy)
+    for copy in h_copies:
+        copy.start()
+    b_copy = pltpu.make_async_copy(basis_hbm.at[0], basis_v, misc_sem.at[1])
+    b_copy.start()
+
+    sent = []
+
+    def forward(block, peer):
+        slot = len(sent)
+        copy = to_band(hx.at[block], hx.at[block], f_send.at[slot], f_recv.at[block], peer)
+        copy.start()
+        sent.append(copy)
+
+    def arrived(block, peer):
+        to_band(hx.at[block], hx.at[block], f_send.at[0], f_recv.at[block], peer).wait_recv()
+
+    y_peer, core_peer = ident(z, 1 - y, core), ident(z, y, 1 - core)
+    for copy in h_across:
+        copy.wait_recv()
+    for k in range(1, nz):
+        forward(b, ident((z + k) % nz, y, core))
+    forward(b, y_peer)
+    forward(b, core_peer)
+    for k in range(1, nz):
+        block = ident((z - k + nz) % nz, y, core)
+        arrived(block, block)
+        forward(block, y_peer)
+        forward(block, core_peer)
+    for k in range(nz):
+        block = ident((z - k + nz) % nz, 1 - y, core)
+        arrived(block, y_peer)
+        forward(block, core_peer)
+    for k in range(nz):
+        for yy in (y, 1 - y):
+            arrived(ident((z - k + nz) % nz, yy, 1 - core), core_peer)
+
+    n_across.wait_recv()
+    nx_copy = pltpu.make_async_copy(nx_v, nx, misc_sem.at[2])
+    nx_copy.start()
+    n_copy.wait()
+    nx_copy.wait()
+    for copy in h_copies:
+        copy.wait()
+
+    def image(blocks, table, e, cross, near, far):
+        row = jnp.concatenate([blocks[e, k] for k in range(6)], axis=1)
+        parts = [near[lax.rem(table[e, k], elements)] for k in range(5)]
+        parts.append(far[lax.rem(table[e, cross], elements)])
+        return jnp.dot(row, jnp.concatenate(parts, axis=0), preferred_element_type=jnp.float32)
+
+    out_copies = []
+    for i, (lo, n) in enumerate(spans):
+        c_copies[i].wait()
+        c_across[i].wait_recv()
+
+        def first_own(e, carry):
+            got = image(hown, nown, e, own_cross, cown[i], cx[i])
+            f1o[i][e] = ((got - center * cown[i][e].astype(jnp.float32)) * (1.0 / half_width)).astype(jnp.bfloat16)
+            return carry
+
+        def first_x(e, carry):
+            got = image(hx, nx, e, x_cross, cx[i], cown[i])
+            f1x[i][e] = ((got - center * cx[i][e].astype(jnp.float32)) * (1.0 / half_width)).astype(jnp.bfloat16)
+            return carry
+
+        start = pl.multiple_of(b * nbl + lo, 128)
+        weight = (1 + occ_ref[:, pl.ds(start, n)]).astype(jnp.float32)
+
+        def second(e, carry):
+            got = image(hown, nown, e, own_cross, f1o[i], f1x[i])
+            once = f1o[i][e].astype(jnp.float32)
+            value = (got - center * once) * (2.0 / half_width) - cown[i][e].astype(jnp.float32)
+            value = value.astype(jnp.bfloat16)
+            outv[i][e] = value
+            scaled = (value.astype(jnp.float32) * weight).astype(jnp.bfloat16)
+            part = lax.dot_general(scaled, value, (((1,), (1,)), ((), ())), preferred_element_type=jnp.float32)
+            if i > 0:
+                part = gram[e] + part
+            if i == count - 1:
+                gsend[e] = part.astype(jnp.bfloat16)
+            gram[e] = part
+            return carry
+
+        lax.fori_loop(0, elements, first_own, 0)
+        lax.fori_loop(0, elements, first_x, 0)
+        lax.fori_loop(0, elements, second, 0)
+        copy = pltpu.make_async_copy(outv[i], filt_hbm.at[:, :, pl.ds(lo, n)], lo_sem.at[i])
+        copy.start()
+        out_copies.append(copy)
+
+    g_copies = []
+    for k in range(1, nb):
+        peer = (b + k) % nb
+        copy = to_band(gsend.at[peer], grecv.at[k], g_send.at[k], g_recv.at[k], peer)
+        copy.start()
+        g_copies.append(copy)
+    b_copy.wait()
+    total = gram[b]
+    for k in range(1, nb):
+        g_copies[k - 1].wait_recv()
+        total = total + grecv[k].astype(jnp.float32)
+    total = total * (1.0 / (2.0 * nbl * nb))
+    high = total.astype(jnp.bfloat16)
+    low = (total - high.astype(jnp.float32)).astype(jnp.bfloat16)
+    functions = basis_v[...]
+    image_g = jnp.dot(functions, high, preferred_element_type=jnp.float32)
+    image_g = image_g + jnp.dot(functions, low, preferred_element_type=jnp.float32)
+    product = image_g * functions.astype(jnp.float32)
+    top = product.astype(jnp.bfloat16)
+    rest = (product - top.astype(jnp.float32)).astype(jnp.bfloat16)
+    ones = jnp.ones((16, product.shape[1]), jnp.bfloat16)
+    over_last = (((1,), (1,)), ((), ()))
+    density = lax.dot_general(ones, top, over_last, preferred_element_type=jnp.float32)
+    density = density + lax.dot_general(ones, rest, over_last, preferred_element_type=jnp.float32)
+    dens_ref[...] = density[0:1]
+
+    for copy in h_across + [n_across] + c_across + sent + g_copies:
+        copy.wait_send()
+    for copy in out_copies:
+        copy.wait()
+
+
+def plane_body(nb, coeffs, hamilton, neighbors, basis, occupation):
+    elements, nbasis, nbl = coeffs.shape
+    points = basis.shape[1]
+    spans, lo = [], 0
+    while lo < nbl:
+        n = min(256, nbl - lo)
+        spans.append((lo, n))
+        lo += n
+    count = len(spans)
+    table = jnp.pad(neighbors, ((0, 0), (0, 128 - neighbors.shape[1])))
+    values = [pltpu.VMEM((elements, nbasis, n), jnp.bfloat16) for _, n in spans]
+    dma = pltpu.SemaphoreType.DMA
+    hbm = pl.BlockSpec(memory_space=pl.ANY)
+    vmem = pl.BlockSpec(memory_space=pltpu.VMEM)
+    forwards = (nb // 4 - 1) + 2 + 2 * (nb // 4 - 1) + nb // 4
+    return pl.pallas_call(
+        functools.partial(kernel, spans, nb),
+        out_shape=(
+            jax.ShapeDtypeStruct(coeffs.shape, jnp.bfloat16),
+            jax.ShapeDtypeStruct((1, points), jnp.float32),
+        ),
+        in_specs=[hbm, hbm, hbm, hbm, vmem],
+        out_specs=(hbm, vmem),
+        scratch_shapes=values * 5 + [
+            pltpu.VMEM((elements, 6, nbasis, nbasis), jnp.bfloat16),
+            pltpu.VMEM((elements, 6, nbasis, nbasis), jnp.bfloat16),
+            pltpu.VMEM((points, nbasis), jnp.bfloat16),
+            pltpu.VMEM((elements, 128), jnp.int32),
+            pltpu.SMEM((elements, 128), jnp.int32),
+            pltpu.SMEM((elements, 128), jnp.int32),
+            pltpu.VMEM((elements, nbasis, nbasis), jnp.float32),
+            pltpu.VMEM((elements, nbasis, nbasis), jnp.bfloat16),
+            pltpu.VMEM((nb, nbasis, nbasis), jnp.bfloat16),
+            dma((count,)), dma((count,)),
+            dma((2,)), dma((2,)),
+            dma((1,)), dma((1,)),
+            dma((forwards,)), dma((nb,)),
+            dma((nb,)), dma((nb,)),
+            dma((count,)), dma((2,)), dma((count,)), dma((3,)),
+        ],
+        compiler_params=pltpu.CompilerParams(collective_id=0, has_side_effects=True),
+    )(coeffs, hamilton, table, basis, occupation.reshape(1, -1))
+
+
 def solution(mesh):
+    layers, nb = mesh.shape["layer"], mesh.shape["band"]
+
+    def body(coeffs, hamilton, neighbors, basis, occupation):
+        elements = coeffs.shape[0]
+        one_kernel = (
+            layers == 2 and elements == FY * FZ and nb == elements
+            and nb % 4 == 0 and coeffs.shape[2] % 128 == 0 and basis.shape[0] == 1
+        )
+        if one_kernel:
+            return plane_body(nb, coeffs, hamilton, neighbors, basis, occupation)
+        return general_body(coeffs, hamilton, neighbors, basis, occupation)
+
     return jax.shard_map(
         body,
         mesh=mesh,

time: 255 us -> 103 us (0.40)
  waiting for transfers between devices: 132 us -> 0 us
  Pallas kernels: 0 us -> 95.6 us
  matrix products: 46.7 us -> 0 us
  local copies, waits for them, and re-layouts: 44 us -> 5.54 us
  starting transfers between devices: 18.3 us -> 0 us
  other arithmetic: 12.7 us -> 0 us
    pallas_call x0 -> x1, Pallas kernels: none -> 95.6 us  [plane_body(): pl.pallas_call(functools.partial(kernel, spans, nb), out_shape=(jax.Shape...]
    ppermute x4 -> x0, waiting for transfers between devices: 75.4 us -> none  [the longest x2 64.8 us: with_halo(): after = lax.ppermute(first, axis, down)]
    all_to_all x1 -> x0, waiting for transfers between devices: 56.2 us -> none  [body(): lax.all_to_all(duplicated, 'band', split_axis=0, concat_axis=2, tiled=True)]
    dot_general x5 -> x0, matrix products: 46.7 us -> none  [the longest x4 35.3 us: neighbor_product(): jnp.einsum('ekij,ekjb->eib', blocks, nearby, preferred_element_type=jnp.f...]
    gather x5 -> x0, local copies, waits for them, and re-layouts: 36 us -> none  [the longest x3 21.3 us: operate(): across = padded[position[:, 5:]] * allowed[:, 5:, None, None]]
    concatenate x2 -> x0, other arithmetic: 12.7 us -> none  [with_halo(): array = jnp.concatenate([before, array, after], axis=dim)]
    ppermute x4 -> x0, starting transfers between devices: 9.39 us -> none  [the longest x2 6.65 us: with_halo(): after = lax.ppermute(first, axis, down)]
    all_to_all x1 -> x0, starting transfers between devices: 8.93 us -> none  [body(): lax.all_to_all(duplicated, 'band', split_axis=0, concat_axis=2, tiled=True)]
  transfers between devices with their start and end apart: 5 -> 0, of which waited for: 5 -> 0; matrix products, arithmetic and copies ran while one was open for 17% -> 0% of each run, Pallas kernels for 0% -> 0%
where the time goes in v1:
time: 103 us; the launch traced here: 102 us
  Pallas kernels  95.6 us (93%)
  local copies, waits for them, and re-layouts  5.54 us (5%)
    pallas_call x1, Pallas kernels, plane_body(): pl.pallas_call(functools.partial(kernel, spans, nb), out_shape=(jax.Shape...  95.6 us
    unnamed x5, local copies, waits for them, and re-layouts  4.94 us

profile of v1, /device:TPU:15, one launch (start us, length us, event | category | flops | bytes accessed | tf_op | source)
XLA Modules:
  0.0 101.8 jit_solution(4078974926102558047)
XLA Ops:
  0.6 0.8 copy.7
  1.4 0.6 pad.4.nbr_hbm
  2.0 95.6 %shard_map.68 = (bf16[16,128,640]{2,1,0:T(8,128)(2,1)}, f32[1,1728]{1,0:T(1,128)}) custom-call(bf16[16,128,640]{2,1,0:T(8,128)(2,1)} %c_hbm.1, bf16[16,7,128,128]{3,2,1,0:T(8,128)(2,1)} %h_hbm.1, s32[16,128]{1,0:T(8,128)} %pad.4.nbr_hbm, bf16[1,1728,128]{2,1,0:T(8,128)(2,1)} %basis_hbm.1, s32[1,10240]{1,0:T(1,128)} %bitcast.1), custom_call_target="tpu_custom_call" | custom-call | tf_op jit(solution)/shard_map/pallas_call | solution.py:259
  97.6 0.0 copy-start
  97.6 3.6 %copy.10 = bf16[16,128,640]{2,1,0:T(8,128)(2,1)} copy(bf16[16,128,640]{2,1,0:T(8,128)(2,1)} %get-tuple-element.4) | data formatting | bytes 5242880
  101.2 0.0 copy-done
  101.2 0.6 copy.11
Async XLA Ops:
  97.6 3.6 %copy-start = (f32[1,1728]{1,0:T(1,128)S(1)}, f32[1,1728]{1,0:T(1,128)}, u32[]{:S(2)}) copy-start(f32[1,1728]{1,0:T(1,128)} %get-tuple-element.5) | copy-start | bytes 20740

commit v2 on v1

--- a/solution.py
+++ b/solution.py
@@ -63,11 +63,11 @@
     return (filtered, density)
 
 
-def kernel(spans, nb, c_hbm, h_hbm, nbr_hbm, basis_hbm, occ_ref, filt_hbm, dens_ref, *scratch):
+def kernel(spans, nb, c_hbm, h_hbm, nbr_hbm, occ_ref, filt_hbm, total_ref, *scratch):
     count = len(spans)
     cown, cx, f1o, f1x, outv = (scratch[i * count:(i + 1) * count] for i in range(5))
-    (hown, hx, basis_v, nx_v, nown, nx, gram, gsend, grecv,
-     c_send, c_recv, hx_send, hx_recv, n_send, n_recv, f_send, f_recv, g_send, g_recv,
+    (hown, hx, nx_v, nown, nx, gram, gsend, gcore, grecv,
+     c_send, c_recv, hx_send, hx_recv, n_send, n_recv, f_send, f_recv, k_send, k_recv, g_send, g_recv,
      lc_sem, lh_sem, lo_sem, misc_sem) = scratch[5 * count:]
     elements = c_hbm.shape[0]
     nbl = c_hbm.shape[2]
@@ -90,9 +90,12 @@
 
     barrier = pltpu.get_barrier_semaphore()
     pl.semaphore_signal(barrier, inc=1, device_id={"layer": other, "band": b}, device_id_type=MESH)
-    for k in range(1, nb):
-        pl.semaphore_signal(barrier, inc=1, device_id={"layer": layer, "band": (b + k) % nb}, device_id_type=MESH)
-    pl.semaphore_wait(barrier, nb)
+    half = nb // 2
+    site = b // 2
+    core_peer = b + 1 - 2 * core
+    for peer in [core_peer] + [(site + k) % half * 2 + core for k in range(1, half)]:
+        pl.semaphore_signal(barrier, inc=1, device_id={"layer": layer, "band": peer}, device_id_type=MESH)
+    pl.semaphore_wait(barrier, half + 1)
 
     def to_x(src, dst, send, recv):
         return pltpu.make_async_remote_copy(
@@ -121,8 +124,6 @@
         c_copies.append(copy)
     for copy in h_copies:
         copy.start()
-    b_copy = pltpu.make_async_copy(basis_hbm.at[0], basis_v, misc_sem.at[1])
-    b_copy.start()
 
     sent = []
 
@@ -135,7 +136,7 @@
     def arrived(block, peer):
         to_band(hx.at[block], hx.at[block], f_send.at[0], f_recv.at[block], peer).wait_recv()
 
-    y_peer, core_peer = ident(z, 1 - y, core), ident(z, y, 1 - core)
+    y_peer = ident(z, 1 - y, core)
     for copy in h_across:
         copy.wait_recv()
     for k in range(1, nz):
@@ -156,7 +157,7 @@
             arrived(ident((z - k + nz) % nz, yy, 1 - core), core_peer)
 
     n_across.wait_recv()
-    nx_copy = pltpu.make_async_copy(nx_v, nx, misc_sem.at[2])
+    nx_copy = pltpu.make_async_copy(nx_v, nx, misc_sem.at[1])
     nx_copy.start()
     n_copy.wait()
     nx_copy.wait()
@@ -174,56 +175,118 @@
         c_copies[i].wait()
         c_across[i].wait_recv()
 
-        def first_own(e, carry):
-            got = image(hown, nown, e, own_cross, cown[i], cx[i])
-            f1o[i][e] = ((got - center * cown[i][e].astype(jnp.float32)) * (1.0 / half_width)).astype(jnp.bfloat16)
-            return carry
-
-        def first_x(e, carry):
-            got = image(hx, nx, e, x_cross, cx[i], cown[i])
-            f1x[i][e] = ((got - center * cx[i][e].astype(jnp.float32)) * (1.0 / half_width)).astype(jnp.bfloat16)
-            return carry
-
+        last = i == count - 1
         start = pl.multiple_of(b * nbl + lo, 128)
         weight = (1 + occ_ref[:, pl.ds(start, n)]).astype(jnp.float32)
 
-        def second(e, carry):
+        def first_own(e):
+            got = image(hown, nown, e, own_cross, cown[i], cx[i])
+            return ((got - center * cown[i][e].astype(jnp.float32)) * (1.0 / half_width)).astype(jnp.bfloat16)
+
+        def first_x(e):
+            got = image(hx, nx, e, x_cross, cx[i], cown[i])
+            return ((got - center * cx[i][e].astype(jnp.float32)) * (1.0 / half_width)).astype(jnp.bfloat16)
+
+        step = 2 if last and elements % 2 == 0 else 1
+
+        def first(t, carry):
+            at = [t * step + u for u in range(step)]
+            mine = [first_own(e) for e in at]
+            theirs = [first_x(e) for e in at]
+            for e, a, c in zip(at, mine, theirs):
+                f1o[i][e] = a
+                f1x[i][e] = c
+            return carry
+
+        def second(e):
             got = image(hown, nown, e, own_cross, f1o[i], f1x[i])
             once = f1o[i][e].astype(jnp.float32)
             value = (got - center * once) * (2.0 / half_width) - cown[i][e].astype(jnp.float32)
             value = value.astype(jnp.bfloat16)
-            outv[i][e] = value
             scaled = (value.astype(jnp.float32) * weight).astype(jnp.bfloat16)
             part = lax.dot_general(scaled, value, (((1,), (1,)), ((), ())), preferred_element_type=jnp.float32)
-            if i > 0:
-                part = gram[e] + part
-            if i == count - 1:
-                gsend[e] = part.astype(jnp.bfloat16)
+            return value, part + gram[e] if i > 0 else part
+
+        def second_plain(e, carry):
+            value, part = second(e)
+            outv[i][e] = value
             gram[e] = part
             return carry
 
-        lax.fori_loop(0, elements, first_own, 0)
-        lax.fori_loop(0, elements, first_x, 0)
-        lax.fori_loop(0, elements, second, 0)
+        def to_core(t):
+            return to_band(gsend.at[2 * t + 1 - core], gcore.at[t], k_send.at[t], k_recv.at[t], core_peer)
+
+        def to_owner(k):
+            element = (site + k) % half * 2 + core
+            return to_band(gsend.at[element], grecv.at[k], g_send.at[k], g_recv.at[k], element)
+
+        def pair_up(s, carry):
+            at = [2 * s, 2 * s + 1]
+            got = [second(2 * t + 1 - core) for t in at]
+            for t, (value, part) in zip(at, got):
+                outv[i][2 * t + 1 - core] = value
+                gsend[2 * t + 1 - core] = part.astype(jnp.bfloat16)
+                to_core(t).start()
+            return carry
+
+        def hand_over(ks):
+            places = [(site + k) % half for k in ks]
+            got = [second(2 * t + core) for t in places]
+            for k, t, (value, part) in zip(ks, places, got):
+                outv[i][2 * t + core] = value
+                to_core(t).wait_recv()
+                part = part + gcore[t].astype(jnp.float32)
+                if isinstance(k, int) and k == half:
+                    gram[2 * t + core] = part
+                else:
+                    gsend[2 * t + core] = part.astype(jnp.bfloat16)
+                    to_owner(k).start()
+
+        def hand_over_two(s, carry):
+            hand_over([2 * s + 1, 2 * s + 2])
+            return carry
+
+        lax.fori_loop(0, elements // step, first, 0)
+        if last:
+            lax.fori_loop(0, half // 2, pair_up, 0)
+            lax.fori_loop(0, half // 2 - 1, hand_over_two, 0)
+            hand_over([half - 1, half])
+        else:
+            lax.fori_loop(0, elements, second_plain, 0)
         copy = pltpu.make_async_copy(outv[i], filt_hbm.at[:, :, pl.ds(lo, n)], lo_sem.at[i])
         copy.start()
         out_copies.append(copy)
 
-    g_copies = []
-    for k in range(1, nb):
-        peer = (b + k) % nb
-        copy = to_band(gsend.at[peer], grecv.at[k], g_send.at[k], g_recv.at[k], peer)
-        copy.start()
-        g_copies.append(copy)
-    b_copy.wait()
     total = gram[b]
-    for k in range(1, nb):
-        g_copies[k - 1].wait_recv()
+    for k in range(1, half):
+        to_owner(k).wait_recv()
         total = total + grecv[k].astype(jnp.float32)
-    total = total * (1.0 / (2.0 * nbl * nb))
+    total_ref[...] = total * (1.0 / (2.0 * nbl * nb))
+
+    for copy in h_across + [n_across] + c_across + sent:
+        copy.wait_send()
+    for t in range(half):
+        to_core(t).wait_send()
+    for k in range(1, half):
+        to_owner(k).wait_send()
+    for copy in out_copies:
+        copy.wait()
+
+
+def finish_kernel(pieces, filt_hbm, total_ref, basis_ref, out_hbm, dens_ref, held, in_sem, out_sem):
+    size = held.shape[0] // pieces
+    spans = [pl.ds(i * size, size) for i in range(pieces)]
+    loads = [pltpu.make_async_copy(filt_hbm.at[at], held.at[at], in_sem.at[i]) for i, at in enumerate(spans)]
+    stores = [pltpu.make_async_copy(held.at[at], out_hbm.at[at], out_sem.at[i]) for i, at in enumerate(spans)]
+    for load in loads:
+        load.start()
+    for load, store in zip(loads, stores):
+        load.wait()
+        store.start()
+    total = total_ref[...]
     high = total.astype(jnp.bfloat16)
     low = (total - high.astype(jnp.float32)).astype(jnp.bfloat16)
-    functions = basis_v[...]
+    functions = basis_ref[0]
     image_g = jnp.dot(functions, high, preferred_element_type=jnp.float32)
     image_g = image_g + jnp.dot(functions, low, preferred_element_type=jnp.float32)
     product = image_g * functions.astype(jnp.float32)
@@ -234,11 +297,8 @@
     density = lax.dot_general(ones, top, over_last, preferred_element_type=jnp.float32)
     density = density + lax.dot_general(ones, rest, over_last, preferred_element_type=jnp.float32)
     dens_ref[...] = density[0:1]
-
-    for copy in h_across + [n_across] + c_across + sent + g_copies:
-        copy.wait_send()
-    for copy in out_copies:
-        copy.wait()
+    for store in stores:
+        store.wait()
 
 
 def plane_body(nb, coeffs, hamilton, neighbors, basis, occupation):
@@ -250,39 +310,51 @@
         spans.append((lo, n))
         lo += n
     count = len(spans)
-    table = jnp.pad(neighbors, ((0, 0), (0, 128 - neighbors.shape[1])))
+    width = neighbors.shape[1]
+    pieces = 4 if elements % 4 == 0 else 1
     values = [pltpu.VMEM((elements, nbasis, n), jnp.bfloat16) for _, n in spans]
     dma = pltpu.SemaphoreType.DMA
     hbm = pl.BlockSpec(memory_space=pl.ANY)
     vmem = pl.BlockSpec(memory_space=pltpu.VMEM)
     forwards = (nb // 4 - 1) + 2 + 2 * (nb // 4 - 1) + nb // 4
+    spread, total = pl.pallas_call(
+        functools.partial(kernel, spans, nb),
+        out_shape=(
+            jax.ShapeDtypeStruct(coeffs.shape, jnp.bfloat16),
+            jax.ShapeDtypeStruct((nbasis, nbasis), jnp.float32),
+        ),
+        in_specs=[hbm, hbm, hbm, vmem],
+        out_specs=(hbm, vmem),
+        scratch_shapes=values * 5 + [
+            pltpu.VMEM((elements, 6, nbasis, nbasis), jnp.bfloat16),
+            pltpu.VMEM((elements, 6, nbasis, nbasis), jnp.bfloat16),
+            pltpu.VMEM((elements, width), jnp.int32),
+            pltpu.SMEM((elements, width), jnp.int32),
+            pltpu.SMEM((elements, width), jnp.int32),
+            pltpu.VMEM((elements, nbasis, nbasis), jnp.float32),
+            pltpu.VMEM((elements, nbasis, nbasis), jnp.bfloat16),
+            pltpu.VMEM((nb // 2, nbasis, nbasis), jnp.bfloat16),
+            pltpu.VMEM((nb // 2, nbasis, nbasis), jnp.bfloat16),
+            dma((count,)), dma((count,)),
+            dma((2,)), dma((2,)),
+            dma((1,)), dma((1,)),
+            dma((forwards,)), dma((nb,)),
+            dma((nb // 2,)), dma((nb // 2,)),
+            dma((nb // 2,)), dma((nb // 2,)),
+            dma((count,)), dma((2,)), dma((count,)), dma((2,)),
+        ],
+        compiler_params=pltpu.CompilerParams(collective_id=0, has_side_effects=True),
+    )(coeffs, hamilton, neighbors, occupation.reshape(1, -1))
     return pl.pallas_call(
-        functools.partial(kernel, spans, nb),
+        functools.partial(finish_kernel, pieces),
         out_shape=(
             jax.ShapeDtypeStruct(coeffs.shape, jnp.bfloat16),
             jax.ShapeDtypeStruct((1, points), jnp.float32),
         ),
-        in_specs=[hbm, hbm, hbm, hbm, vmem],
+        in_specs=[hbm, vmem, vmem],
         out_specs=(hbm, vmem),
-        scratch_shapes=values * 5 + [
-            pltpu.VMEM((elements, 6, nbasis, nbasis), jnp.bfloat16),
-            pltpu.VMEM((elements, 6, nbasis, nbasis), jnp.bfloat16),
-            pltpu.VMEM((points, nbasis), jnp.bfloat16),
-            pltpu.VMEM((elements, 128), jnp.int32),
-            pltpu.SMEM((elements, 128), jnp.int32),
-            pltpu.SMEM((elements, 128), jnp.int32),
-            pltpu.VMEM((elements, nbasis, nbasis), jnp.float32),
-            pltpu.VMEM((elements, nbasis, nbasis), jnp.bfloat16),
-            pltpu.VMEM((nb, nbasis, nbasis), jnp.bfloat16),
-            dma((count,)), dma((count,)),
-            dma((2,)), dma((2,)),
-            dma((1,)), dma((1,)),
-            dma((forwards,)), dma((nb,)),
-            dma((nb,)), dma((nb,)),
-            dma((count,)), dma((2,)), dma((count,)), dma((3,)),
-        ],
-        compiler_params=pltpu.CompilerParams(collective_id=0, has_side_effects=True),
-    )(coeffs, hamilton, table, basis, occupation.reshape(1, -1))
+        scratch_shapes=[pltpu.VMEM(coeffs.shape, jnp.bfloat16), dma((pieces,)), dma((pieces,))],
+    )(spread, total, basis)
 
 
 def solution(mesh):
@@ -292,7 +364,7 @@
         elements = coeffs.shape[0]
         one_kernel = (
             layers == 2 and elements == FY * FZ and nb == elements
-            and nb % 4 == 0 and coeffs.shape[2] % 128 == 0 and basis.shape[0] == 1
+            and nb % 4 == 0 and nb >= 8 and coeffs.shape[2] % 128 == 0 and basis.shape[0] == 1
         )
         if one_kernel:
             return plane_body(nb, coeffs, hamilton, neighbors, basis, occupation)

time: 103 us -> 89.6 us (0.87)
  Pallas kernels: 95.6 us -> 86.1 us
  local copies, waits for them, and re-layouts: 5.54 us -> 1.36 us
    pallas_call x1, Pallas kernels: 95.6 us -> 81.7 us  [plane_body(): pl.pallas_call(functools.partial(kernel, spans, nb), out_shape=(jax.Shape...]
    pallas_call x0 -> x1, Pallas kernels: none -> 4.42 us  [plane_body(): pl.pallas_call(functools.partial(finish_kernel, pieces), out_shape=(jax.S...]
    unnamed x5 -> x1, local copies, waits for them, and re-layouts: 4.94 us -> 1.36 us
where the time goes in v2:
time: 89.6 us; the launch traced here: 88.1 us
  Pallas kernels  86.1 us (96%)
  local copies, waits for them, and re-layouts  1.36 us (2%)
    pallas_call x1, Pallas kernels, plane_body(): pl.pallas_call(functools.partial(kernel, spans, nb), out_shape=(jax.Shape...  81.7 us
    pallas_call x1, Pallas kernels, plane_body(): pl.pallas_call(functools.partial(finish_kernel, pieces), out_shape=(jax.S...  4.42 us

profile of v2, /device:TPU:15, one launch (start us, length us, event | category | flops | bytes accessed | tf_op | source)
XLA Modules:
  0.0 88.1 jit_solution(1254537219270992335)
XLA Ops:
  0.6 1.4 %copy.7.nbr_hbm = s32[16,7]{1,0:T(8,128)} copy(s32[16,7]{0,1:T(8,128)} %param.7) | data formatting | bytes 896 | tf_op args[2]
  2.0 81.7 %shard_map.68 = (bf16[16,128,640]{2,1,0:T(8,128)(2,1)}, f32[128,128]{1,0:T(8,128)}) custom-call(bf16[16,128,640]{2,1,0:T(8,128)(2,1)} %c_hbm.1, bf16[16,7,128,128]{3,2,1,0:T(8,128)(2,1)} %h_hbm.1, s32[16,7]{1,0:T(8,128)} %copy.7.nbr_hbm, s32[1,10240]{1,0:T(1,128)} %bitcast.1), custom_call_target="tpu_custom_call" | custom-call | tf_op jit(solution)/shard_map/pallas_call | solution.py:320
  83.7 4.4 %shard_map.69 = (bf16[16,128,640]{2,1,0:T(8,128)(2,1)}, f32[1,1728]{1,0:T(1,128)}) custom-call(bf16[16,128,640]{2,1,0:T(8,128)(2,1)} %get-tuple-element.4.filt_hbm, f32[128,128]{1,0:T(8,128)} %get-tuple-element.5.total_ref, bf16[1,1728,128]{2,1,0:T(8,128)(2,1)} %basis_ref.1), custom_call_target="tpu_custom_call" | custom-call | tf_op jit(solution)/shard_map/pallas_call | solution.py:348

commit v3 on v2

--- a/solution.py
+++ b/solution.py
@@ -66,7 +66,7 @@
 def kernel(spans, nb, c_hbm, h_hbm, nbr_hbm, occ_ref, filt_hbm, total_ref, *scratch):
     count = len(spans)
     cown, cx, f1o, f1x, outv = (scratch[i * count:(i + 1) * count] for i in range(5))
-    (hown, hx, nx_v, nown, nx, gram, gsend, gcore, grecv,
+    (hown, hx, nx_v, nown, nx, early, gram, gsend, gcore, grecv,
      c_send, c_recv, hx_send, hx_recv, n_send, n_recv, f_send, f_recv, k_send, k_recv, g_send, g_recv,
      lc_sem, lh_sem, lo_sem, misc_sem) = scratch[5 * count:]
     elements = c_hbm.shape[0]
@@ -166,20 +166,34 @@
 
     def image(blocks, table, e, cross, near, far):
         row = jnp.concatenate([blocks[e, k] for k in range(6)], axis=1)
-        parts = [near[lax.rem(table[e, k], elements)] for k in range(5)]
-        parts.append(far[lax.rem(table[e, cross], elements)])
+        parts = [near[lax.rem(table[k, e], elements)] for k in range(5)]
+        parts.append(far[lax.rem(table[cross, e], elements)])
         return jnp.dot(row, jnp.concatenate(parts, axis=0), preferred_element_type=jnp.float32)
 
     out_copies = []
     for i, (lo, n) in enumerate(spans):
         c_copies[i].wait()
+        last = i == count - 1
+
+        def inside(e, carry):
+            row = jnp.concatenate([hown[e, k] for k in range(5)], axis=1)
+            parts = [cown[i][lax.rem(nown[k, e], elements)] for k in range(5)]
+            got = jnp.dot(row, jnp.concatenate(parts, axis=0), preferred_element_type=jnp.float32)
+            early[e] = got - center * cown[i][e].astype(jnp.float32)
+            return carry
+
+        if last:
+            lax.fori_loop(0, elements, inside, 0)
         c_across[i].wait_recv()
 
-        last = i == count - 1
         start = pl.multiple_of(b * nbl + lo, 128)
         weight = (1 + occ_ref[:, pl.ds(start, n)]).astype(jnp.float32)
 
         def first_own(e):
+            if last:
+                across = cx[i][lax.rem(nown[own_cross, e], elements)]
+                got = early[e] + jnp.dot(hown[e, 5], across, preferred_element_type=jnp.float32)
+                return (got * (1.0 / half_width)).astype(jnp.bfloat16)
             got = image(hown, nown, e, own_cross, cown[i], cx[i])
             return ((got - center * cown[i][e].astype(jnp.float32)) * (1.0 / half_width)).astype(jnp.bfloat16)
 
@@ -243,7 +257,7 @@
                     to_owner(k).start()
 
         def hand_over_two(s, carry):
-            hand_over([2 * s + 1, 2 * s + 2])
+            hand_over([half // 2 + s, half // 2 - s - 1])
             return carry
 
         lax.fori_loop(0, elements // step, first, 0)
@@ -273,12 +287,15 @@
         copy.wait()
 
 
-def finish_kernel(pieces, filt_hbm, total_ref, basis_ref, out_hbm, dens_ref, held, in_sem, out_sem):
+def finish_kernel(pieces, filt_hbm, total_ref, basis_hbm, out_hbm, dens_ref, held, basis_v, in_sem, out_sem, basis_sem):
     size = held.shape[0] // pieces
     spans = [pl.ds(i * size, size) for i in range(pieces)]
     loads = [pltpu.make_async_copy(filt_hbm.at[at], held.at[at], in_sem.at[i]) for i, at in enumerate(spans)]
     stores = [pltpu.make_async_copy(held.at[at], out_hbm.at[at], out_sem.at[i]) for i, at in enumerate(spans)]
-    for load in loads:
+    basis_copy = pltpu.make_async_copy(basis_hbm.at[0], basis_v, basis_sem.at[0])
+    loads[0].start()
+    basis_copy.start()
+    for load in loads[1:]:
         load.start()
     for load, store in zip(loads, stores):
         load.wait()
@@ -286,7 +303,8 @@
     total = total_ref[...]
     high = total.astype(jnp.bfloat16)
     low = (total - high.astype(jnp.float32)).astype(jnp.bfloat16)
-    functions = basis_ref[0]
+    basis_copy.wait()
+    functions = basis_v[...]
     image_g = jnp.dot(functions, high, preferred_element_type=jnp.float32)
     image_g = image_g + jnp.dot(functions, low, preferred_element_type=jnp.float32)
     product = image_g * functions.astype(jnp.float32)
@@ -311,7 +329,7 @@
         lo += n
     count = len(spans)
     width = neighbors.shape[1]
-    pieces = 4 if elements % 4 == 0 else 1
+    pieces = 8 if elements % 8 == 0 else 1
     values = [pltpu.VMEM((elements, nbasis, n), jnp.bfloat16) for _, n in spans]
     dma = pltpu.SemaphoreType.DMA
     hbm = pl.BlockSpec(memory_space=pl.ANY)
@@ -328,9 +346,10 @@
         scratch_shapes=values * 5 + [
             pltpu.VMEM((elements, 6, nbasis, nbasis), jnp.bfloat16),
             pltpu.VMEM((elements, 6, nbasis, nbasis), jnp.bfloat16),
-            pltpu.VMEM((elements, width), jnp.int32),
-            pltpu.SMEM((elements, width), jnp.int32),
-            pltpu.SMEM((elements, width), jnp.int32),
+            pltpu.VMEM((width, elements), jnp.int32),
+            pltpu.SMEM((width, elements), jnp.int32),
+            pltpu.SMEM((width, elements), jnp.int32),
+            pltpu.VMEM((elements, nbasis, spans[-1][1]), jnp.float32),
             pltpu.VMEM((elements, nbasis, nbasis), jnp.float32),
             pltpu.VMEM((elements, nbasis, nbasis), jnp.bfloat16),
             pltpu.VMEM((nb // 2, nbasis, nbasis), jnp.bfloat16),
@@ -344,16 +363,20 @@
             dma((count,)), dma((2,)), dma((count,)), dma((2,)),
         ],
         compiler_params=pltpu.CompilerParams(collective_id=0, has_side_effects=True),
-    )(coeffs, hamilton, neighbors, occupation.reshape(1, -1))
+    )(coeffs, hamilton, neighbors.T, occupation.reshape(1, -1))
     return pl.pallas_call(
         functools.partial(finish_kernel, pieces),
         out_shape=(
             jax.ShapeDtypeStruct(coeffs.shape, jnp.bfloat16),
             jax.ShapeDtypeStruct((1, points), jnp.float32),
         ),
-        in_specs=[hbm, vmem, vmem],
+        in_specs=[hbm, vmem, hbm],
         out_specs=(hbm, vmem),
-        scratch_shapes=[pltpu.VMEM(coeffs.shape, jnp.bfloat16), dma((pieces,)), dma((pieces,))],
+        scratch_shapes=[
+            pltpu.VMEM(coeffs.shape, jnp.bfloat16),
+            pltpu.VMEM((points, nbasis), jnp.bfloat16),
+            dma((pieces,)), dma((pieces,)), dma((1,)),
+        ],
     )(spread, total, basis)
 
 

time: 89.6 us -> 90.4 us (level)
  the two profiles are of different devices: /device:TPU:15 before, /device:TPU:17 now
where the time goes in v3:
time: 90.4 us; the launch traced here: 90.1 us
  Pallas kernels  89.5 us (99%)
    pallas_call x1, Pallas kernels, plane_body(): pl.pallas_call(functools.partial(kernel, spans, nb), out_shape=(jax.Shape...  85.1 us
    pallas_call x1, Pallas kernels, plane_body(): pl.pallas_call(functools.partial(finish_kernel, pieces), out_shape=(jax.S...  4.41 us

profile of v3, /device:TPU:17, one launch (start us, length us, event | category | flops | bytes accessed | tf_op | source)
XLA Modules:
  0.0 90.1 jit_solution(4473734822169871983)
XLA Ops:
  0.6 85.1 %shard_map.68 = (bf16[16,128,640]{2,1,0:T(8,128)(2,1)}, f32[128,128]{1,0:T(8,128)}) custom-call(bf16[16,128,640]{2,1,0:T(8,128)(2,1)} %c_hbm.1, bf16[16,7,128,128]{3,2,1,0:T(8,128)(2,1)} %h_hbm.1, s32[7,16]{1,0:T(8,128)} %bitcast.3, s32[1,10240]{1,0:T(1,128)} %bitcast.2), custom_call_target="tpu_custom_call" | custom-call | tf_op jit(solution)/shard_map/pallas_call | solution.py:338
  85.7 4.4 %shard_map.69 = (bf16[16,128,640]{2,1,0:T(8,128)(2,1)}, f32[1,1728]{1,0:T(1,128)}) custom-call(bf16[16,128,640]{2,1,0:T(8,128)(2,1)} %get-tuple-element.4.filt_hbm, f32[128,128]{1,0:T(8,128)} %get-tuple-element.5.total_ref, bf16[1,1728,128]{2,1,0:T(8,128)(2,1)} %basis_hbm.1), custom_call_target="tpu_custom_call" | custom-call | tf_op jit(solution)/shard_map/pallas_call | solution.py:367

commit v4 on v2

--- a/solution.py
+++ b/solution.py
@@ -166,8 +166,8 @@
 
     def image(blocks, table, e, cross, near, far):
         row = jnp.concatenate([blocks[e, k] for k in range(6)], axis=1)
-        parts = [near[lax.rem(table[e, k], elements)] for k in range(5)]
-        parts.append(far[lax.rem(table[e, cross], elements)])
+        parts = [near[lax.rem(table[k, e], elements)] for k in range(5)]
+        parts.append(far[lax.rem(table[cross, e], elements)])
         return jnp.dot(row, jnp.concatenate(parts, axis=0), preferred_element_type=jnp.float32)
 
     out_copies = []
@@ -207,10 +207,12 @@
             part = lax.dot_general(scaled, value, (((1,), (1,)), ((), ())), preferred_element_type=jnp.float32)
             return value, part + gram[e] if i > 0 else part
 
-        def second_plain(e, carry):
-            value, part = second(e)
-            outv[i][e] = value
-            gram[e] = part
+        def second_plain(s, carry):
+            at = [2 * s, 2 * s + 1]
+            got = [second(e) for e in at]
+            for e, (value, part) in zip(at, got):
+                outv[i][e] = value
+                gram[e] = part
             return carry
 
         def to_core(t):
@@ -252,7 +254,7 @@
             lax.fori_loop(0, half // 2 - 1, hand_over_two, 0)
             hand_over([half - 1, half])
         else:
-            lax.fori_loop(0, elements, second_plain, 0)
+            lax.fori_loop(0, elements // 2, second_plain, 0)
         copy = pltpu.make_async_copy(outv[i], filt_hbm.at[:, :, pl.ds(lo, n)], lo_sem.at[i])
         copy.start()
         out_copies.append(copy)
@@ -328,9 +330,9 @@
         scratch_shapes=values * 5 + [
             pltpu.VMEM((elements, 6, nbasis, nbasis), jnp.bfloat16),
             pltpu.VMEM((elements, 6, nbasis, nbasis), jnp.bfloat16),
-            pltpu.VMEM((elements, width), jnp.int32),
-            pltpu.SMEM((elements, width), jnp.int32),
-            pltpu.SMEM((elements, width), jnp.int32),
+            pltpu.VMEM((width, elements), jnp.int32),
+            pltpu.SMEM((width, elements), jnp.int32),
+            pltpu.SMEM((width, elements), jnp.int32),
             pltpu.VMEM((elements, nbasis, nbasis), jnp.float32),
             pltpu.VMEM((elements, nbasis, nbasis), jnp.bfloat16),
             pltpu.VMEM((nb // 2, nbasis, nbasis), jnp.bfloat16),
@@ -344,7 +346,7 @@
             dma((count,)), dma((2,)), dma((count,)), dma((2,)),
         ],
         compiler_params=pltpu.CompilerParams(collective_id=0, has_side_effects=True),
-    )(coeffs, hamilton, neighbors, occupation.reshape(1, -1))
+    )(coeffs, hamilton, neighbors.T, occupation.reshape(1, -1))
     return pl.pallas_call(
         functools.partial(finish_kernel, pieces),
         out_shape=(

time: 89.6 us -> 87.6 us (0.978)
  local copies, waits for them, and re-layouts: 1.36 us -> 0 us
    unnamed x1 -> x0, local copies, waits for them, and re-layouts: 1.36 us -> none
where the time goes in v4:
time: 87.6 us; the launch traced here: 86.2 us
  Pallas kernels  85.5 us (98%)
    pallas_call x1, Pallas kernels, plane_body(): pl.pallas_call(functools.partial(kernel, spans, nb), out_shape=(jax.Shape...  81.1 us
    pallas_call x1, Pallas kernels, plane_body(): pl.pallas_call(functools.partial(finish_kernel, pieces), out_shape=(jax.S...  4.42 us

profile of v4, /device:TPU:15, one launch (start us, length us, event | category | flops | bytes accessed | tf_op | source)
XLA Modules:
  0.0 86.2 jit_solution(14075954367161675911)
XLA Ops:
  0.6 81.1 %shard_map.68 = (bf16[16,128,640]{2,1,0:T(8,128)(2,1)}, f32[128,128]{1,0:T(8,128)}) custom-call(bf16[16,128,640]{2,1,0:T(8,128)(2,1)} %c_hbm.1, bf16[16,7,128,128]{3,2,1,0:T(8,128)(2,1)} %h_hbm.1, s32[7,16]{1,0:T(8,128)} %bitcast.3, s32[1,10240]{1,0:T(1,128)} %bitcast.2), custom_call_target="tpu_custom_call" | custom-call | tf_op jit(solution)/shard_map/pallas_call | solution.py:322
  81.7 4.4 %shard_map.69 = (bf16[16,128,640]{2,1,0:T(8,128)(2,1)}, f32[1,1728]{1,0:T(1,128)}) custom-call(bf16[16,128,640]{2,1,0:T(8,128)(2,1)} %get-tuple-element.4.filt_hbm, f32[128,128]{1,0:T(8,128)} %get-tuple-element.5.total_ref, bf16[1,1728,128]{2,1,0:T(8,128)(2,1)} %basis_ref.1), custom_call_target="tpu_custom_call" | custom-call | tf_op jit(solution)/shard_map/pallas_call | solution.py:350
